TPU v7x, 512 devices: a whole 4x4x16 slice. The times are simulated.
512 devices in a mesh: segment: 4 (over x_hi, core), seq: 32 (over x_lo, z), dp: 4 (over y).
Axes of the slice: x: 4 (x_hi: 2, x_lo: 2; x = x_hi * 2 + x_lo), y: 4, z: 16, core: 2. Of those that a mesh axis runs over, the one named last changes fastest.
Arguments:
- q_in: bfloat16 [4, 4096, 1536], P('dp', 'seq', 'segment'), may hold values from -128 to 128
- k_in: bfloat16 [4, 4096, 1536], P('dp', 'seq', 'segment'), may hold values from -128 to 128
- v_in: bfloat16 [4, 4096, 1536], P('dp', 'seq', 'segment'), may hold values from -6 to 6
- q_gain: float32 [2, 64], replicated, may hold values from 1.5 to 4
- gate: float32 [768], replicated, may hold values from -6 to 6
- cot: bfloat16 [4, 4096, 768], P('dp', 'seq'), may hold values from -6 to 6
Outputs:
- attn_out: bfloat16 [4, 4096, 1536], P('dp', 'seq', 'segment')
- grad_gate: float32 [768], replicated
All inputs are finite; a program needn't handle non-finite values.
Results may differ from a plain program's by a relative error of at most 0.028.
The roundings to bfloat16 on the way count: a program that leaves them out, or rounds other values in their place, can miss the bound.
Values may be sent and summed in bfloat16 or wider, within the bound.
A program may use at most 64 MiB of HBM per device.

v0:
```python
import jax
import jax.numpy as jnp
from jax import lax
from jax.sharding import PartitionSpec as P

HEAD_DIM = 64


def shifted(value, axis, steps):
    count = lax.axis_size(axis)
    first, last = (max(0, -steps), min(count, count - steps))
    return lax.ppermute(value, axis, [(source, source + steps) for source in range(first, last)])


def attend(query, all_keys, all_values):
    count_rows = query.shape[0]
    total_keys = all_keys.shape[0]
    span = 2 * HEAD_DIM
    pieces = []
    probs_list = []
    totals_list = []
    for offset in range(0, query.shape[1], span):
        query_group = query[:, offset : offset + span].reshape(count_rows, 2, HEAD_DIM)
        keys_group = all_keys[:, offset : offset + span].reshape(total_keys, 2, HEAD_DIM)
        values_group = all_values[:, offset : offset + span].reshape(total_keys, 2, HEAD_DIM)
        scores = jnp.einsum(
            "qhd,khd->hqk", query_group, keys_group, preferred_element_type=jnp.float32
        ) * HEAD_DIM ** (-0.5)
        peak = jnp.max(scores, axis=-1, keepdims=True)
        expd = jnp.exp(scores - peak)
        total = jnp.sum(expd, axis=-1, keepdims=True)
        probs = expd.astype(jnp.bfloat16)
        result = jnp.einsum("hqk,khd->qhd", probs, values_group, preferred_element_type=jnp.float32)
        result = result / jnp.transpose(total, (1, 0, 2))
        pieces.append(result.reshape(count_rows, span))
        probs_list.append(probs)
        totals_list.append(total)
    return (jnp.concatenate(pieces, axis=1), probs_list, totals_list)


def attend_back(probs_list, totals_list, normed, upstream, all_keys, all_values):
    count_rows = upstream.shape[0]
    total_keys = all_keys.shape[0]
    span = 2 * HEAD_DIM
    pieces = []
    for number in range(len(probs_list)):
        offset = number * span
        upstream_group = upstream[:, offset : offset + span].reshape(count_rows, 2, HEAD_DIM)
        normed_group = normed[:, offset : offset + span].reshape(count_rows, 2, HEAD_DIM)
        keys_group = all_keys[:, offset : offset + span].reshape(total_keys, 2, HEAD_DIM)
        values_group = all_values[:, offset : offset + span].reshape(total_keys, 2, HEAD_DIM)
        dprob = jnp.einsum(
            "qhd,khd->hqk", upstream_group, values_group, preferred_element_type=jnp.float32
        )
        delta = jnp.sum(upstream_group.astype(jnp.float32) * normed_group, axis=-1)
        delta = jnp.transpose(delta, (1, 0))[:, :, None]
        dscore = (
            probs_list[number].astype(jnp.float32) / totals_list[number] * (dprob - delta)
        ).astype(jnp.bfloat16)
        result = jnp.einsum(
            "hqk,khd->qhd", dscore, keys_group, preferred_element_type=jnp.float32
        ) * HEAD_DIM ** (-0.5)
        pieces.append(result.reshape(count_rows, span))
    return jnp.concatenate(pieces, axis=1)


def local(q_in, k_in, v_in, q_gain, gate, cot):
    half = lax.axis_size("segment") // 2
    place = lax.axis_index("segment")
    is_main = place >= half
    section = place // half
    slot = place % half
    queries = q_in[0]
    keys = k_in[0]
    values = v_in[0]
    count_rows = queries.shape[0]
    width_dev = queries.shape[1]
    all_keys, all_values = (
        lax.all_gather(keys, "seq", axis=0, tiled=True),
        lax.all_gather(values, "seq", axis=0, tiled=True),
    )
    gain_row = lax.dynamic_slice_in_dim(q_gain, section, 1, 0)[0]
    gate_part = lax.dynamic_slice_in_dim(gate, slot * width_dev, width_dev, 0)
    cot_part = lax.dynamic_slice_in_dim(cot[0], slot * width_dev, width_dev, 1)
    raw = queries.astype(jnp.float32).reshape(count_rows, width_dev // HEAD_DIM, HEAD_DIM)
    unit = raw * lax.rsqrt(jnp.mean(raw * raw, axis=-1, keepdims=True) + 1e-06)
    base = (unit * gain_row).reshape(count_rows, width_dev)

    def control_run(base_in):
        normed_c = attend(base_in.astype(jnp.bfloat16), all_keys, all_values)[0]
        return lax.optimization_barrier(normed_c.astype(jnp.bfloat16))

    def control_skip(base_in):
        return jnp.zeros((count_rows, width_dev), jnp.bfloat16)

    first = lax.cond(is_main, control_skip, control_run, base)
    first_wide = first.astype(jnp.float32)
    outgoing = (gate_part * first_wide).astype(jnp.bfloat16)
    incoming = shifted(outgoing, "segment", half)

    def main_run(incoming_in):
        query = (base + incoming_in.astype(jnp.float32)).astype(jnp.bfloat16)
        normed_m, probs_list, totals_list = attend(query, all_keys, all_values)
        dquery = attend_back(probs_list, totals_list, normed_m, cot_part, all_keys, all_values)
        return (normed_m.astype(jnp.bfloat16), dquery)

    def main_skip(incoming_in):
        return (
            jnp.zeros((count_rows, width_dev), jnp.bfloat16),
            jnp.zeros((count_rows, width_dev), jnp.float32),
        )

    final, dquery_main = lax.cond(is_main, main_run, main_skip, incoming)
    returned = shifted(dquery_main.astype(jnp.bfloat16), "segment", -half)
    returned_wide = returned.astype(jnp.float32)
    part_gate = jnp.sum(first_wide * returned_wide, axis=0)
    placed = lax.dynamic_update_slice_in_dim(
        jnp.zeros((width_dev * half,), jnp.float32), part_gate, slot * width_dev, 0
    )
    total_gate = lax.psum(placed, ("segment", "seq", "dp"))
    output = jnp.where(is_main, final, first)
    return (output[None], total_gate)


def solution(mesh):
    in_specs = (
        P("dp", "seq", "segment"),
        P("dp", "seq", "segment"),
        P("dp", "seq", "segment"),
        P(),
        P(),
        P("dp", "seq", None),
    )
    out_specs = (P("dp", "seq", "segment"), P())
    return jax.shard_map(local, mesh=mesh, in_specs=in_specs, out_specs=out_specs, check_vma=False)
```

profile of v0, /device:TPU:1, one launch (start us, length us, event | category | flops | bytes accessed | tf_op | source)
XLA Modules:
  0.0 449.7 jit_solution(1224437534765963869)
XLA Ops:
  7.2 0.0 copy-start
  7.2 0.0 all-gather.5.cloned.1.call-start
  7.2 1.6 copy.10
  8.9 0.0 all-gather.5.cloned.1.call-update
  8.9 0.0 all-gather.7.cloned.1.call-start
  8.9 1.6 copy.11
  10.6 0.0 all-gather.7.cloned.1.call-update
  10.6 0.0 copy-done
  10.6 0.1 mul.127
  10.7 1.0 copy.9
  11.8 0.1 fusion.70
  11.9 0.8 dynamic_slice.11
  12.7 116.3 %all-gather.5.cloned.1.call-done = bf16[1,4096,384]{1,2,0:T(8,128)(2,1)} async-done(((bf16[1,128,384]{1,2,0:T(8,128)(2,1)}), bf16[1,4096,384]{1,2,0:T(8,128)(2,1)}) %all-gather.5.cloned.1.call-update) | async-done | bytes 3145744 | tf_op jit(solution)/shard_map/all_gather | solution.py:79
  129.0 133.1 %all-gather.7.cloned.1.call-done = bf16[1,4096,384]{1,2,0:T(8,128)(2,1)} async-done(((bf16[1,128,384]{1,2,0:T(8,128)(2,1)}), bf16[1,4096,384]{1,2,0:T(8,128)(2,1)}) %all-gather.7.cloned.1.call-update) | async-done | bytes 3145744 | tf_op jit(solution)/shard_map/all_gather | solution.py:80
  262.1 10.9 %conditional.2 = (f32[128,384]{0,1:T(8,128)S(1)}, bf16[128,384]{1,0:T(8,128)(2,1)S(1)}) conditional(s32[]{:T(128)} %convert_element_type.105, (f32[128,384]{0,1:T(8,128)S(1)}, bf16[4096,384]{0,1:T(8,128)(2,1)}, bf16[4096,384]{0,1:T(8,128)(2,1)}) %tuple.81, () %tuple.30), branch_computations={%region_1.8_spmd, %region_8.9_spmd} | conditional | flops 824670720 | bytes 58014736 | solution.py:96
  262.1 3.2 fusion.71
  265.4 0.8 fusion.76
  266.2 0.7 fusion
  267.0 0.9 fusion.39
  267.9 0.8 fusion.75
  268.7 0.7 fusion.2
  269.4 0.9 fusion.36
  270.4 0.8 fusion.74
  271.2 0.7 fusion.4
  271.9 0.9 fusion.33
  272.9 0.1 copy.15
  273.1 0.0 copy-start.6
  273.1 0.1 multiply_convert_fusion
  273.2 1.3 collective-permute-start
  274.5 1.6 collective-permute-done
  276.1 0.0 copy-done.6
  276.1 0.9 conditional.3
  276.1 0.7 broadcast.53.clone
  277.0 1.3 collective-permute-start.1
  278.3 1.6 select_bitcast_fusion
  279.8 38.2 %collective-permute-done.1 = bf16[128,384]{0,1:T(8,128)(2,1)S(1)} collective-permute-done((bf16[128,384]{0,1:T(8,128)(2,1)S(1)}, bf16[128,384]{0,1:T(8,128)(2,1)S(1)}, u32[]{:S(2)}, u32[]{:S(2)}) %collective-permute-start.1) | collective-permute-done | bytes 98336 | tf_op jit(solution)/shard_map/ppermute | solution.py:12
  318.0 0.1 multiply_reduce_fusion.3
  318.2 0.2 dynamic_update_slice.3
  318.5 124.4 %psum.7 = f32[768]{0:T(1024)} all-reduce(f32[768]{0:T(1024)S(1)} %dynamic_update_slice.3), channel_id=1, replica_groups=mesh['segment'=4,'seq'=32,'dp'=4] {'segment','seq','dp'}, use_global_device_ids=true, to_apply=%region_21.22 | all-reduce | flops 768 | bytes 6144 | tf_op jit(solution)/shard_map/psum | solution.py:120
  (11 shorter events, 0.1 us)
Async XLA Ops:
  7.2 3.4 copy-start
  7.2 121.8 %all-gather.5.cloned.1.call-start = ((), (), s32[]{:S(2)}) async-start(), calls=%async_computation | async-start | bytes 3244032 | tf_op jit(solution)/shard_map/all_gather | solution.py:79
  8.9 253.3 %all-gather.7.cloned.1.call-start = ((), (), s32[]{:S(2)}) async-start(), calls=%async_computation.1 | async-start | bytes 3244032 | tf_op jit(solution)/shard_map/all_gather | solution.py:80
  273.1 3.1 copy-start.6
  273.2 2.9 collective-permute-start
  277.0 41.1 %collective-permute-start.1 = (bf16[128,384]{0,1:T(8,128)(2,1)S(1)}, bf16[128,384]{0,1:T(8,128)(2,1)S(1)}, u32[]{:S(2)}, u32[]{:S(2)}) collective-permute-start(bf16[128,384]{0,1:T(8,128)(2,1)S(1)} %get-tuple-element.53), channel_id=1, source_target_pairs={{256,0},{384,128},{257,1},{385,129},{258,2},{386,130},{259,3},{387... | collective-permute-start | bytes 294920 | tf_op jit(solution)/shard_map/ppermute | solution.py:12
Sparse Core Ops, SparseCore 0:
  10.6 118.3 all-gather.4
  131.0 131.0 all-gather.6
where the time goes:
time: 450 us
  waiting for transfers between devices  289 us (64%)
  blocking collectives  124 us (28%)
  between operations  14.2 us (3%)
  local copies, waits for them, and re-layouts  9.4 us (2%)
  matrix products  5.29 us (1%)
    all_gather x1, waiting for transfers between devices, local(): lax.all_gather(values, 'seq', axis=0, tiled=True)  133 us
    psum x1, blocking collectives, local(): total_gate = lax.psum(placed, ('segment', 'seq', 'dp'))  124 us
    all_gather x1, waiting for transfers between devices, local(): lax.all_gather(keys, 'seq', axis=0, tiled=True)  116 us
    ppermute x2, waiting for transfers between devices, shifted(): lax.ppermute(value, axis, [(source, source + steps) for source in range(f...  39.8 us
  transfers between devices with their start and end apart: 4, of which 4 were waited for; matrix products, arithmetic and copies ran while one was open for 1% of the time, Pallas kernels for 0%

commit v1 on v0

--- a/solution.py
+++ b/solution.py
@@ -117,7 +117,8 @@
     placed = lax.dynamic_update_slice_in_dim(
         jnp.zeros((width_dev * half,), jnp.float32), part_gate, slot * width_dev, 0
     )
-    total_gate = lax.psum(placed, ("segment", "seq", "dp"))
+    middle = lax.psum(placed, "segment")
+    total_gate = lax.psum(middle, ("seq", "dp"))
     output = jnp.where(is_main, final, first)
     return (output[None], total_gate)
 

time: 450 us -> 664 us (1.48)
  the two profiles are of different devices: /device:TPU:1 before, /device:TPU:2 now
where the time goes in v1:
time: 664 us
  blocking collectives  316 us (48%)
  waiting for transfers between devices  312 us (47%)
  between operations  14.2 us (2%)
  local copies, waits for them, and re-layouts  9.4 us (1%)
    psum x1, blocking collectives, local(): total_gate = lax.psum(middle, ('seq', 'dp'))  308 us
    all_gather x1, waiting for transfers between devices, local(): lax.all_gather(keys, 'seq', axis=0, tiled=True)  137 us
    all_gather x1, waiting for transfers between devices, local(): lax.all_gather(values, 'seq', axis=0, tiled=True)  133 us
    ppermute x2, waiting for transfers between devices, shifted(): lax.ppermute(value, axis, [(source, source + steps) for source in range(f...  41.6 us
  transfers between devices with their start and end apart: 4, of which 4 were waited for; matrix products, arithmetic and copies ran while one was open for 1% of the time, Pallas kernels for 0%

profile of v1, /device:TPU:2, one launch (start us, length us, event | category | flops | bytes accessed | tf_op | source)
XLA Modules:
  0.0 663.8 jit_solution(7789718472452773892)
XLA Ops:
  7.2 0.0 copy-start
  7.2 0.0 all-gather.5.cloned.1.call-start
  7.2 1.6 copy.10
  8.9 0.0 all-gather.5.cloned.1.call-update
  8.9 0.0 all-gather.7.cloned.1.call-start
  8.9 1.6 copy.11
  10.6 0.0 all-gather.7.cloned.1.call-update
  10.6 0.0 copy-done
  10.6 0.1 mul.127
  10.7 1.0 copy.9
  11.8 0.1 fusion.70
  11.9 0.8 dynamic_slice.11
  12.7 137.4 %all-gather.5.cloned.1.call-done = bf16[1,4096,384]{1,2,0:T(8,128)(2,1)} async-done(((bf16[1,128,384]{1,2,0:T(8,128)(2,1)}), bf16[1,4096,384]{1,2,0:T(8,128)(2,1)}) %all-gather.5.cloned.1.call-update) | async-done | bytes 3145744 | tf_op jit(solution)/shard_map/all_gather | solution.py:79
  150.1 133.1 %all-gather.7.cloned.1.call-done = bf16[1,4096,384]{1,2,0:T(8,128)(2,1)} async-done(((bf16[1,128,384]{1,2,0:T(8,128)(2,1)}), bf16[1,4096,384]{1,2,0:T(8,128)(2,1)}) %all-gather.7.cloned.1.call-update) | async-done | bytes 3145744 | tf_op jit(solution)/shard_map/all_gather | solution.py:80
  283.2 10.9 %conditional.2 = (f32[128,384]{0,1:T(8,128)S(1)}, bf16[128,384]{1,0:T(8,128)(2,1)S(1)}) conditional(s32[]{:T(128)} %convert_element_type.105, (f32[128,384]{0,1:T(8,128)S(1)}, bf16[4096,384]{0,1:T(8,128)(2,1)}, bf16[4096,384]{0,1:T(8,128)(2,1)}) %tuple.81, () %tuple.30), branch_computations={%region_1.8_spmd, %region_8.9_spmd} | conditional | flops 824670720 | bytes 58014736 | solution.py:96
  283.2 3.2 fusion.71
  286.5 0.8 fusion.76
  287.3 0.7 fusion
  288.1 0.9 fusion.39
  289.0 0.8 fusion.75
  289.8 0.7 fusion.2
  290.6 0.9 fusion.36
  291.5 0.8 fusion.74
  292.3 0.7 fusion.4
  293.0 0.9 fusion.33
  294.0 0.1 copy.15
  294.2 0.0 copy-start.6
  294.2 0.1 multiply_convert_fusion
  294.3 1.3 collective-permute-start
  295.6 2.2 collective-permute-done
  297.8 0.0 copy-done.6
  297.8 0.9 conditional.3
  297.8 0.7 broadcast.53.clone
  298.6 1.3 collective-permute-start.1
  299.9 1.6 select_bitcast_fusion
  301.5 39.4 %collective-permute-done.1 = bf16[128,384]{0,1:T(8,128)(2,1)S(1)} collective-permute-done((bf16[128,384]{0,1:T(8,128)(2,1)S(1)}, bf16[128,384]{0,1:T(8,128)(2,1)S(1)}, u32[]{:S(2)}, u32[]{:S(2)}) %collective-permute-start.1) | collective-permute-done | bytes 98336 | tf_op jit(solution)/shard_map/ppermute | solution.py:12
  340.9 0.1 multiply_reduce_fusion.3
  341.0 0.2 dynamic_update_slice.3
  341.3 7.2 %psum.14 = f32[768]{0:T(1024)S(1)} all-reduce(f32[768]{0:T(1024)S(1)} %dynamic_update_slice.3), channel_id=1, replica_groups=mesh['segment'=4,'seq'=32,'dp'=4] {'segment'}, use_global_device_ids=true, to_apply=%region_21.22 | all-reduce | flops 768 | bytes 6144 | tf_op jit(solution)/shard_map/psum | solution.py:120
  348.5 308.4 %psum.15 = f32[768]{0:T(1024)} all-reduce(f32[768]{0:T(1024)S(1)} %psum.14), channel_id=1, replica_groups=mesh['segment'=4,'seq'=32,'dp'=4] {'seq','dp'}, use_global_device_ids=true, to_apply=%region_22.23 | all-reduce | flops 768 | bytes 6144 | tf_op jit(solution)/shard_map/psum | solution.py:121
  (11 shorter events, 0.1 us)
Async XLA Ops:
  7.2 3.4 copy-start
  7.2 143.0 %all-gather.5.cloned.1.call-start = ((), (), s32[]{:S(2)}) async-start(), calls=%async_computation | async-start | bytes 3244032 | tf_op jit(solution)/shard_map/all_gather | solution.py:79
  8.9 274.4 %all-gather.7.cloned.1.call-start = ((), (), s32[]{:S(2)}) async-start(), calls=%async_computation.1 | async-start | bytes 3244032 | tf_op jit(solution)/shard_map/all_gather | solution.py:80
  294.2 3.6 copy-start.6
  294.3 3.5 collective-permute-start
  298.6 42.3 %collective-permute-start.1 = (bf16[128,384]{0,1:T(8,128)(2,1)S(1)}, bf16[128,384]{0,1:T(8,128)(2,1)S(1)}, u32[]{:S(2)}, u32[]{:S(2)}) collective-permute-start(bf16[128,384]{0,1:T(8,128)(2,1)S(1)} %get-tuple-element.53), channel_id=1, source_target_pairs={{256,0},{384,128},{257,1},{385,129},{258,2},{386,130},{259,3},{387... | collective-permute-start | bytes 294920 | tf_op jit(solution)/shard_map/ppermute | solution.py:12
Sparse Core Ops, SparseCore 0:
  10.6 139.4 all-gather.4
  152.1 131.0 all-gather.6
